TPU v7x, 32 devices: a whole 2x2x4 slice. The times are simulated.
32 devices in a mesh: dp: 4 (over z), tx: 2 (over y), ty: 4 (over x, core).
Axes of the slice: x: 2, y: 2, z: 4, core: 2. Of those that a mesh axis runs over, the one named last changes fastest.
Arguments:
- inputs: bfloat16 [8, 1024, 2048], P('dp', 'ty'), may hold values from -6 to 6
- lengths: int32 [8], replicated, may hold values from 1 to 1024, 5120 in all
- prompt_deal: int32 [8], replicated, may hold values from 0 to 7, each once
- block_owner: int32 [4], replicated, may hold values from 0 to 3, each once
- attn_gain: float32 [2048], replicated, may hold values from 0.5 to 1.5
- latent_gain: float32 [512], replicated, may hold values from 0.5 to 1.5
- final_gain: float32 [2048], replicated, may hold values from 0.5 to 1.5
- w_query: float32 [2048, 3072], P('dp', ('tx', 'ty')), may hold values from -4 to 4
- w_down_kv: float32 [2048, 576], P('dp'), may hold values from -0.125 to 0.125
- w_up_kv: float32 [512, 4096], P('dp', ('tx', 'ty')), may hold values from -4 to 4
- w_out: float32 [2048, 2048], P('dp', 'tx'), may hold values from -0.125 to 0.125
- w_vocab: float32 [2048, 57344], P('dp', ('tx', 'ty')), may hold values from -0.125 to 0.125
Outputs:
- hidden_out: bfloat16 [8, 1024, 2048], P('dp', 'ty', 'tx')
- logits: float32 [8, 57344], P('dp', ('tx', 'ty'))
Inputs may be any that keep to these rules, and one draw needn't show every extreme that they name: `prompt_deal`: a permutation of the 8 prompts. `block_owner`: a permutation of the 4 row blocks. `lengths`: some prompt has exactly 1024 live tokens.
All inputs are finite; a program needn't handle non-finite values.
Results may differ from a plain program's by a relative error of at most 0.0065.
The roundings to bfloat16 on the way count: a program that leaves them out, or rounds other values in their place, can miss the bound.
Values may be sent and summed in bfloat16 or wider, within the bound.
A program may use at most 192 MiB of HBM per device.

v0:
```python
import jax
import jax.numpy as jnp
from jax import lax
from jax.sharding import PartitionSpec as P

NOPE = 128
ROPE = 64
LATENT = 512
LEN = 1024
EPS = 1e-06


def normalize(values, gain):
    wide = values.astype(jnp.float32)
    return wide * lax.rsqrt(jnp.mean(wide * wide, axis=-1, keepdims=True) + EPS) * gain


def rotate(values, position):
    half_dim = values.shape[-1] // 2
    frequency = 10000.0 ** (-jnp.arange(half_dim, dtype=jnp.float32) / half_dim)
    angles = position.astype(jnp.float32)[..., None] * frequency
    cosine = jnp.cos(angles)
    sine = jnp.sin(angles)
    first_half = values[..., :half_dim]
    second_half = values[..., half_dim:]
    return jnp.concatenate(
        [first_half * cosine - second_half * sine, first_half * sine + second_half * cosine],
        axis=-1,
    )


def shards(
    inputs,
    lengths,
    prompt_deal,
    block_owner,
    attn_gain,
    latent_gain,
    final_gain,
    w_query,
    w_down_kv,
    w_up_kv,
    w_out,
    w_vocab,
):
    groups = lax.axis_size("dp")
    inverse = (
        jnp.zeros((groups,), jnp.int32).at[block_owner].set(jnp.arange(groups, dtype=jnp.int32))
    )

    def arrange(gathered):
        block_rows = gathered.shape[0] // groups
        blocks = gathered.reshape((groups, block_rows) + gathered.shape[1:])
        return jnp.take(blocks, inverse, axis=0).reshape(gathered.shape)

    query_w, down_w, up_w, out_w = (
        lax.all_gather(w_query.astype(jnp.bfloat16), "dp", axis=0, tiled=True),
        lax.all_gather(w_down_kv.astype(jnp.bfloat16), "dp", axis=0, tiled=True),
        lax.all_gather(w_up_kv.astype(jnp.bfloat16), "dp", axis=0, tiled=True),
        lax.all_gather(w_out.astype(jnp.bfloat16), "dp", axis=0, tiled=True),
    )
    query_w = arrange(query_w)
    down_w = arrange(down_w)
    up_w = arrange(up_w)
    out_w = arrange(out_w)
    query_w, up_w = (
        lax.all_gather(query_w, "ty", axis=1, tiled=True),
        lax.all_gather(up_w, "ty", axis=1, tiled=True),
    )
    per_grp, quarter, width = inputs.shape
    heads = query_w.shape[1] // (NOPE + ROPE)
    position = lax.axis_index("ty") * quarter + jnp.arange(quarter, dtype=jnp.int32)
    slots = lax.axis_index("dp") * per_grp + jnp.arange(per_grp, dtype=jnp.int32)
    live_len = jnp.take(lengths, jnp.take(prompt_deal, slots))
    flat_rows = inputs.reshape(per_grp * quarter, width)
    normed = normalize(flat_rows, attn_gain).astype(jnp.bfloat16)
    queries = jnp.dot(normed, query_w, preferred_element_type=jnp.float32).reshape(
        per_grp, quarter, heads, NOPE + ROPE
    )
    queries = jnp.concatenate(
        [queries[..., :NOPE], rotate(queries[..., NOPE:], position[None, :, None])], axis=-1
    ).astype(jnp.bfloat16)
    down_proj = jnp.dot(normed, down_w, preferred_element_type=jnp.float32).reshape(
        per_grp, quarter, LATENT + ROPE
    )
    latent = normalize(down_proj[..., :LATENT], latent_gain).astype(jnp.bfloat16)
    key_rope = rotate(down_proj[..., LATENT:], position[None, :]).astype(jnp.bfloat16)
    gathered = lax.all_gather(
        jnp.concatenate([latent, key_rope], axis=-1), "ty", axis=1, tiled=True
    )
    key_val = jnp.dot(gathered[..., :LATENT], up_w, preferred_element_type=jnp.float32).astype(
        jnp.bfloat16
    )
    rope_all = gathered[..., LATENT:]
    key_val = key_val.reshape(per_grp, LEN, heads, 2, NOPE)
    key_nope = key_val[:, :, :, 0]
    values = key_val[:, :, :, 1]
    score_scale = (NOPE + ROPE) ** (-0.5)
    scores = (
        jnp.einsum(
            "pqhd,pkhd->phqk", queries[..., :NOPE], key_nope, preferred_element_type=jnp.float32
        )
        + jnp.einsum(
            "pqhd,pkd->phqk", queries[..., NOPE:], rope_all, preferred_element_type=jnp.float32
        )
    ) * score_scale
    key_pos = jnp.arange(LEN, dtype=jnp.int32)
    allowed = (key_pos[None, None, :] <= position[None, :, None]) & (
        key_pos[None, None, :] < live_len[:, None, None]
    )
    scores = jnp.where(allowed[:, None], scores, -1e30)
    top = jnp.max(scores, axis=-1, keepdims=True)
    expo = jnp.exp(scores - top)
    softmax_w = (expo / jnp.sum(expo, axis=-1, keepdims=True)).astype(jnp.bfloat16)
    attended = jnp.einsum(
        "phqk,pkhd->pqhd", softmax_w, values, preferred_element_type=jnp.float32
    ).astype(jnp.bfloat16)
    attended = attended.reshape(per_grp * quarter, heads * NOPE)
    own_width = width // lax.axis_size("tx")
    col_start = lax.axis_index("tx") * own_width
    partial_value = lax.dot_general(
        attended, out_w, (((1,), (1,)), ((), ())), preferred_element_type=jnp.float32
    ).reshape(per_grp, quarter, width)
    summed = lax.psum_scatter(partial_value, "tx", scatter_dimension=2, tiled=True)
    residual = lax.dynamic_slice_in_dim(inputs, col_start, own_width, 2)
    layer_out = (residual.astype(jnp.float32) + summed).astype(jnp.bfloat16)
    selector = (position[None, :] == (live_len - 1)[:, None]).astype(jnp.float32)
    picked = jnp.einsum("pq,pqd->pd", selector, layer_out.astype(jnp.float32))
    placed = lax.dynamic_update_slice_in_dim(
        jnp.zeros((per_grp, width), jnp.float32), picked, col_start, 1
    )
    last_rows = lax.psum(placed, ("tx", "ty"))
    final_rows = normalize(last_rows, final_gain).astype(jnp.bfloat16)
    vocab_block = arrange(lax.all_gather(w_vocab.astype(jnp.bfloat16), "dp", axis=0, tiled=True))
    logits = jnp.dot(final_rows, vocab_block, preferred_element_type=jnp.float32)
    return (layer_out, logits)


def solution(mesh):
    placed = (
        P("dp", "ty", None),
        P(),
        P(),
        P(),
        P(),
        P(),
        P(),
        P("dp", ("tx", "ty")),
        P("dp", None),
        P("dp", ("tx", "ty")),
        P("dp", "tx"),
        P("dp", ("tx", "ty")),
    )
    return jax.shard_map(
        shards,
        mesh=mesh,
        in_specs=placed,
        out_specs=(P("dp", "ty", "tx"), P("dp", ("tx", "ty"))),
        check_vma=False,
    )
```

profile of v0, /device:TPU:0, one launch (start us, length us, event | category | flops | bytes accessed | tf_op | source)
XLA Modules:
  0.0 1004.1 jit_solution(8479508930206960993)
XLA Ops:
  7.2 2.2 convert_element_type.73
  9.6 1.9 convert_element_type.78
  11.6 2.9 convert_element_type.82
  14.6 0.6 scatter_custom_fusion
  15.2 24.1 %all_gather.26 = bf16[512,512]{1,0:T(8,128)(2,1)S(1)} all-gather(bf16[128,512]{1,0:T(8,128)(2,1)S(1)} %convert_element_type.76), channel_id=1, replica_groups=mesh['dp'=4,'tx'=2,'ty'=4] {'dp'}, dimensions={0}, use_global_device_ids=true | all-gather | bytes 655360 | tf_op jit(solution)/shard_map/all_gather | solution.py:59
  39.3 0.6 gather_fusion.1
  39.9 1.0 bitcast_select_fusion.1
  41.1 0.5 fusion.4
  41.8 27.0 %all-gather.8.cloned.1.call-done = bf16[2048,576]{0,1:T(8,128)(2,1)} async-done(((bf16[512,576]{0,1:T(8,128)(2,1)}), bf16[2048,576]{0,1:T(8,128)(2,1)}) %all-gather.8.cloned.1.call-update) | async-done | bytes 2359312 | tf_op jit(solution)/shard_map/all_gather | solution.py:58
  68.8 1.9 copy.68
  70.7 2.2 gather_fusion
  72.9 2.1 copy.58
  75.2 1.5 fusion.8
  77.0 0.9 pad_maximum_fusion.1
  77.9 29.3 %all-gather.14.cloned.1.call-done = bf16[2048,384]{1,0:T(8,128)(2,1)} async-done(((bf16[512,384]{1,0:T(8,128)(2,1)}), bf16[2048,384]{1,0:T(8,128)(2,1)}) %all-gather.14.cloned.1.call-update) | async-done | bytes 1572880 | tf_op jit(solution)/shard_map/all_gather | solution.py:57
  107.3 2.3 gather_fusion.2
  109.6 0.8 copy.54
  110.4 1.3 broadcast_select_fusion.1
  111.8 0.6 gather_fusion.8
  112.5 0.6 gather_fusion.9
  113.7 75.4 %all-gather.18.cloned.1.call-done = bf16[2048,1024]{1,0:T(8,128)(2,1)} async-done(((bf16[512,1024]{1,0:T(8,128)(2,1)}), bf16[2048,1024]{1,0:T(8,128)(2,1)}) %all-gather.18.cloned.1.call-update) | async-done | bytes 4194320 | tf_op jit(solution)/shard_map/all_gather | solution.py:60
  189.1 4.9 gather_fusion.3
  194.0 4.9 broadcast_select_fusion
  198.9 12.8 %all-gather.12.cloned.1.call-done = bf16[512,2048]{1,0:T(8,128)(2,1)} async-done(((bf16[512,512]{1,0:T(8,128)(2,1)}), bf16[512,2048]{1,0:T(8,128)(2,1)}) %all-gather.12.cloned.1.call-update) | async-done | bytes 2097168 | tf_op jit(solution)/shard_map/all_gather | solution.py:68
  211.7 25.8 %all-gather.10.cloned.1.call-done = bf16[2,1024,576]{1,2,0:T(8,128)(2,1)} async-done(((bf16[2,256,576]{1,2,0:T(8,128)(2,1)}), bf16[2,1024,576]{1,2,0:T(8,128)(2,1)}) %all-gather.10.cloned.1.call-update) | async-done | bytes 2359312 | tf_op jit(solution)/shard_map/all_gather | solution.py:88
  237.5 10.7 %convolution_convert_fusion = bf16[2,1024,2048]{2,1,0:T(8,128)(2,1)} fusion(bf16[2,1024,576]{1,2,0:T(8,128)(2,1)} %all-gather.10.cloned.1.call-done, bf16[512,2048]{1,0:T(8,128)(2,1)} %all-gather.12.cloned.1.call-done), kind=kOutput, calls=%fused_computation.20 | convolution fusion | flops 4299161600 | bytes 12582912 | tf_op jit(solution)/shard_map/dot_general | solution.py:91
  248.1 14.5 %reshape.344 = bf16[2,1024,8,2,128]{4,3,2,1,0:T(2,128)(2,1)} reshape(bf16[2,1024,2048]{2,1,0:T(8,128)(2,1)} %convolution_convert_fusion) | data formatting | bytes 16777216 | tf_op jit(solution)/shard_map/reshape | solution.py:95
  262.6 17.5 %fusion.36 = (bf16[2,1024,8,1,128]{4,3,2,1,0:T(2,128)(2,1)}, bf16[2,1024,8,1,128]{4,3,2,1,0:T(2,128)(2,1)}) fusion(bf16[2,1024,8,2,128]{4,3,2,1,0:T(2,128)(2,1)} %reshape.344), kind=kLoop, calls=%fused_computation.93 | loop fusion | bytes 16777216 | tf_op jit(solution)/shard_map/slice | solution.py:97
  280.1 20.1 %copy.55 = bf16[2,1024,8,1,128]{1,4,2,0,3:T(8,128)(2,1)} copy(bf16[2,1024,8,1,128]{4,3,2,1,0:T(2,128)(2,1)} %get-tuple-element.9) | data formatting | bytes 8388608
  300.2 5.7 fusion.13
  306.0 1.6 copy-done.8
  307.8 9.1 fusion.22
  316.8 17.3 %fusion.37 = (f32[2,8,256]{2,1,0:T(8,128)S(1)}, f32[2,8,256,1024]{3,2,1,0:T(8,128)}) fusion(f32[2,1024,256,8]{1,2,3,0:T(8,128)} %fusion.22, pred[2,256,1024]{2,1,0:T(8,128)(4,1)S(1)} %broadcast_and_fusion, bf16[2,1024,8,1,128]{4,3,2,1,0:T(2,128)(2,1)} %get-tuple-element.10, f32[2,256,8,192]{1,3,2,0:T(8,128)} %copy-done.8), kind=kOutput, calls=%fused_computation.94 | convolution fusion | flops 1094714368 | bytes 43532288 | tf_op jit(solution)/shard_map/sub | solution.py:113
  334.1 8.8 fusion.18
  342.9 4.4 fusion.38
  347.4 9.2 convert_element_type.85
  356.7 45.0 %reduce-scatter.2.cloned.1.call-done = f32[2,256,1024]{2,1,0:T(8,128)} async-done(((f32[2,256,2048]{2,1,0:T(8,128)}), f32[2,256,1024]{2,1,0:T(8,128)}) %reduce-scatter.2.cloned.1.call-update) | async-done | bytes 2097168 | tf_op jit(solution)/shard_map/reduce_scatter | solution.py:124
  401.7 2.0 add_convert_fusion
  404.0 23.1 %psum.7 = f32[2,2048]{1,0:T(2,128)S(1)} all-reduce(f32[2,2048]{1,0:T(2,128)S(1)} %bitcast_dynamic-update-slice_fusion), channel_id=1, replica_groups=mesh['dp'=4,'tx'=2,'ty'=4] {'tx','ty'}, use_global_device_ids=true, to_apply=%region_6.8 | all-reduce | flops 4096 | bytes 32768 | tf_op jit(solution)/shard_map/psum | solution.py:132
  427.2 469.4 %all-gather.20.cloned.1.call-done = bf16[2048,7168]{1,0:T(8,128)(2,1)} async-done(((bf16[512,7168]{1,0:T(8,128)(2,1)}), bf16[2048,7168]{1,0:T(8,128)(2,1)}) %all-gather.20.cloned.1.call-update) | async-done | bytes 29360144 | tf_op jit(solution)/shard_map/all_gather | solution.py:134
  896.5 20.0 %fusion.35 = (bf16[4,512,1792]{2,1,0:T(8,128)(2,1)}, bf16[4,512,1792]{2,1,0:T(8,128)(2,1)}, bf16[4,512,1792]{2,1,0:T(8,128)(2,1)}, bf16[4,512,1792]{2,1,0:T(8,128)(2,1)}) fusion(bf16[4,512,7168]{2,1,0:T(8,128)(2,1)} %bitcast.74), kind=kLoop, calls=%fused_computation.92 | loop fusion | bytes 58720256 | tf_op jit(solution)/shard_map/jit(_take)/gather | solution.py:54
  916.6 7.1 gather_fusion.7
  923.7 7.0 gather_fusion.6
  930.7 7.0 gather_fusion.5
  937.8 7.1 gather_fusion.4
  944.9 20.2 %pad_maximum_fusion = bf16[4,512,7168]{2,1,0:T(8,128)(2,1)} fusion(bf16[4,512,1792]{2,1,0:T(8,128)(2,1)} %gather_fusion.7, bf16[4,512,1792]{2,1,0:T(8,128)(2,1)} %gather_fusion.6, bf16[4,512,1792]{2,1,0:T(8,128)(2,1)} %gather_fusion.5, bf16[4,512,1792]{2,1,0:T(8,128)(2,1)} %gather_fusion.4), kind=kLoop, calls=%fused_computation.12 | loop fusion | flops 117440512 | bytes 58720256
  965.1 20.2 %bitcast_select_fusion = bf16[2048,7168]{1,0:T(8,128)(2,1)} fusion(bf16[4,512,7168]{2,1,0:T(8,128)(2,1)} %pad_maximum_fusion, pred[2048]{0:T(1024)(128)(4,1)S(1)} %bitcast.86), kind=kLoop, calls=%fused_computation.13 | loop fusion | flops 14680064 | bytes 58722304 | tf_op jit(solution)/shard_map/jit(_take)/select_n | solution.py:54
  985.3 12.0 %fusion.26 = f32[2,7168]{1,0:T(2,128)} fusion(bf16[2048,7168]{1,0:T(8,128)(2,1)} %bitcast_select_fusion, f32[2,2048]{1,0:T(2,128)S(1)} %psum.7, f32[2]{0:T(128)S(1)} %add_rsqrt_fusion.2, f32[2048]{0:T(1024)S(1)} %copy-done.10), kind=kOutput, calls=%fused_computation.62 | convolution fusion | flops 58732544 | bytes 29442056 | tf_op jit(solution)/shard_map/dot_general | solution.py:135
  (76 shorter events, 2.7 us)
Async XLA Ops:
  7.2 104.6 %copy-start = (s32[8]{0:T(128)S(1)}, s32[8]{0:T(128)}, u32[]{:S(2)}) copy-start(s32[8]{0:T(128)} %param.16) | copy-start | bytes 100
  7.2 7.3 copy-start.9
  7.2 7.3 copy-start.13
  7.2 61.6 %all-gather.8.cloned.1.call-start = ((), (), s32[]{:S(2)}) async-start(), calls=%async_computation.1 | async-start | bytes 2949120 | tf_op jit(solution)/shard_map/all_gather | solution.py:58
  9.5 97.8 %all-gather.14.cloned.1.call-start = ((), (), s32[]{:S(2)}) async-start(), calls=%async_computation.4 | async-start | bytes 1966080 | tf_op jit(solution)/shard_map/all_gather | solution.py:57
  11.5 29.6 %copy-start.3 = (bf16[2,256,2048]{2,1,0:T(8,128)(2,1)S(1)}, bf16[2,256,2048]{2,1,0:T(8,128)(2,1)}, u32[]{:S(2)}) copy-start(bf16[2,256,2048]{2,1,0:T(8,128)(2,1)} %param.14) | copy-start | bytes 6291460
  11.5 177.6 %all-gather.18.cloned.1.call-start = ((), (), s32[]{:S(2)}) async-start(), calls=%async_computation.6 | async-start | bytes 5242880 | tf_op jit(solution)/shard_map/all_gather | solution.py:60
  14.4 197.2 %all-gather.12.cloned.1.call-start = ((), (), s32[]{:S(2)}) async-start(), calls=%async_computation.3 | async-start | bytes 2621440 | tf_op jit(solution)/shard_map/all_gather | solution.py:68
  40.9 196.5 %all-gather.10.cloned.1.call-start = ((), (), s32[]{:S(2)}) async-start(), calls=%async_computation.2 | async-start | bytes 2949120 | tf_op jit(solution)/shard_map/all_gather | solution.py:88
  70.7 4.3 copy-start.12
  72.9 2.3 copy-start.4
  75.2 1.7 copy-start.11
  77.9 222.3 %all-gather.16.cloned.1.call-start = ((), (), s32[]{:S(2)}) async-start(), calls=%async_computation.5 | async-start | bytes 7864320 | tf_op jit(solution)/shard_map/all_gather | solution.py:67
  109.6 2.9 copy-start.2
  111.7 290.0 %reduce-scatter.2.cloned.1.call-start = ((), (), s32[]{:S(2)}) async-start(), calls=%async_computation.7 | async-start | bytes 6291456 | tf_op jit(solution)/shard_map/reduce_scatter | solution.py:124
  280.1 20.1 %copy-start.5 = (bf16[2,256,2048]{2,1,0:T(8,128)(2,1)S(1)}, bf16[2,256,2048]{2,1,0:T(8,128)(2,1)}, u32[]{:S(2)}) copy-start(bf16[2,256,2048]{2,1,0:T(8,128)(2,1)} %param.14) | copy-start | bytes 6291460
  305.9 1.6 copy-start.8
  334.1 8.8 copy-start.7
  347.3 549.2 %all-gather.20.cloned.1.call-start = ((), (), s32[]{:S(2)}) async-start(), calls=%async_computation.8 | async-start | bytes 36700160 | tf_op jit(solution)/shard_map/all_gather | solution.py:134
  403.7 512.9 %copy-start.6 = (bf16[2,256,1024]{2,1,0:T(8,128)(2,1)}, bf16[2,256,1024]{2,1,0:T(8,128)(2,1)S(1)}, u32[]{:S(2)}) copy-start(bf16[2,256,1024]{2,1,0:T(8,128)(2,1)S(1)} %add_convert_fusion) | copy-start | bytes 3145732
  965.1 20.2 %copy-start.10 = (f32[2048]{0:T(1024)S(1)}, f32[2048]{0:T(1024)}, u32[]{:S(2)}) copy-start(f32[2048]{0:T(1024)} %param.20) | copy-start | bytes 24580
  985.2 12.0 %copy-start.1 = (s32[8]{0:T(128)S(1)}, s32[8]{0:T(128)}, u32[]{:S(2)}) copy-start(s32[8]{0:T(128)} %param.16) | copy-start | bytes 100
Sparse Core Ops, SparseCore 0:
  9.6 59.1 all-gather.7
  70.4 36.8 all-gather.13
  109.4 79.6 all-gather.17
  190.5 21.1 all-gather.11
  213.1 24.3 all-gather.9
  238.9 46.3 all-gather.15
  347.4 54.2 reduce-scatter.1
  403.4 493.1 all-gather.19
where the time goes:
time: 1010 us; the launch traced here: 1000 us
  waiting for transfers between devices  685 us (68%)
  local copies, waits for them, and re-layouts  119 us (12%)
  matrix products  69.7 us (7%)
  other arithmetic  68.5 us (7%)
  blocking collectives  47.2 us (5%)
  between operations  14.5 us (1%)
    all_gather x1, waiting for transfers between devices, shards(): lax.all_gather(w_vocab.astype(jnp.bfloat16), 'dp', axis=0, tiled=True)  469 us
    all_gather x1, waiting for transfers between devices, shards(): lax.all_gather(w_out.astype(jnp.bfloat16), 'dp', axis=0, tiled=True)  75.4 us
    gather x11, local copies, waits for them, and re-layouts, arrange(): return jnp.take(blocks, inverse, axis=0).reshape(gathered.shape)  61.2 us
    reduce_scatter x1, waiting for transfers between devices, shards(): lax.psum_scatter(partial_value, 'tx', scatter_dimension=2, tiled=True)  45 us
    all_gather x1, waiting for transfers between devices, shards(): lax.all_gather(w_query.astype(jnp.bfloat16), 'dp', axis=0, tiled=True)  29.3 us
    select_n x5, other arithmetic, arrange(): return jnp.take(blocks, inverse, axis=0).reshape(gathered.shape)  27.3 us
    all_gather x1, waiting for transfers between devices, shards(): lax.all_gather(w_down_kv.astype(jnp.bfloat16), 'dp', axis=0, tiled=True)  27 us
    all_gather x1, waiting for transfers between devices, shards(): lax.all_gather(jnp.concatenate([latent, key_rope], axis=-1), 'ty', axis=1...  25.8 us
  transfers between devices with their start and end apart: 8, of which 7 were waited for; matrix products, arithmetic and copies ran while one was open for 11% of the time, Pallas kernels for 0%

commit v1 on v0

--- a/solution.py
+++ b/solution.py
@@ -129,7 +129,7 @@
     placed = lax.dynamic_update_slice_in_dim(
         jnp.zeros((per_grp, width), jnp.float32), picked, col_start, 1
     )
-    last_rows = lax.psum(placed, ("tx", "ty"))
+    last_rows = lax.psum(lax.psum(placed, "ty"), "tx")
     final_rows = normalize(last_rows, final_gain).astype(jnp.bfloat16)
     vocab_block = arrange(lax.all_gather(w_vocab.astype(jnp.bfloat16), "dp", axis=0, tiled=True))
     logits = jnp.dot(final_rows, vocab_block, preferred_element_type=jnp.float32)

time: 1010 us -> 1010 us (level)
    psum x1 -> x2, blocking collectives: 23.1 us -> 18.4 us  [shards(): last_rows = lax.psum(lax.psum(placed, 'ty'), 'tx')]
where the time goes in v1:
time: 1010 us; the launch traced here: 1000 us
  waiting for transfers between devices  689 us (68%)
  local copies, waits for them, and re-layouts  119 us (12%)
  matrix products  69.7 us (7%)
  other arithmetic  68.7 us (7%)
  blocking collectives  42.5 us (4%)
  between operations  14.5 us (1%)
    all_gather x1, waiting for transfers between devices, shards(): lax.all_gather(w_vocab.astype(jnp.bfloat16), 'dp', axis=0, tiled=True)  474 us
    all_gather x1, waiting for transfers between devices, shards(): lax.all_gather(w_out.astype(jnp.bfloat16), 'dp', axis=0, tiled=True)  75.4 us
    gather x11, local copies, waits for them, and re-layouts, arrange(): return jnp.take(blocks, inverse, axis=0).reshape(gathered.shape)  61.2 us
    reduce_scatter x1, waiting for transfers between devices, shards(): lax.psum_scatter(partial_value, 'tx', scatter_dimension=2, tiled=True)  45 us
    all_gather x1, waiting for transfers between devices, shards(): lax.all_gather(w_query.astype(jnp.bfloat16), 'dp', axis=0, tiled=True)  29.3 us
    select_n x5, other arithmetic, arrange(): return jnp.take(blocks, inverse, axis=0).reshape(gathered.shape)  27.4 us
    all_gather x1, waiting for transfers between devices, shards(): lax.all_gather(w_down_kv.astype(jnp.bfloat16), 'dp', axis=0, tiled=True)  27 us
    all_gather x1, waiting for transfers between devices, shards(): lax.all_gather(jnp.concatenate([latent, key_rope], axis=-1), 'ty', axis=1...  25.8 us
  transfers between devices with their start and end apart: 8, of which 7 were waited for; matrix products, arithmetic and copies ran while one was open for 11% of the time, Pallas kernels for 0%

profile of v1, /device:TPU:0, one launch (start us, length us, event | category | flops | bytes accessed | tf_op | source)
XLA Modules:
  0.0 1004.2 jit_solution(5274765796002045988)
XLA Ops:
  7.2 2.2 convert_element_type.73
  9.6 1.9 convert_element_type.78
  11.6 2.9 convert_element_type.82
  14.6 0.6 scatter_custom_fusion
  15.2 24.1 %all_gather.26 = bf16[512,512]{1,0:T(8,128)(2,1)S(1)} all-gather(bf16[128,512]{1,0:T(8,128)(2,1)S(1)} %convert_element_type.76), channel_id=1, replica_groups=mesh['dp'=4,'tx'=2,'ty'=4] {'dp'}, dimensions={0}, use_global_device_ids=true | all-gather | bytes 655360 | tf_op jit(solution)/shard_map/all_gather | solution.py:59
  39.3 0.6 gather_fusion.1
  40.0 1.0 bitcast_select_fusion.1
  41.8 27.0 %all-gather.8.cloned.1.call-done = bf16[2048,576]{0,1:T(8,128)(2,1)} async-done(((bf16[512,576]{0,1:T(8,128)(2,1)}), bf16[2048,576]{0,1:T(8,128)(2,1)}) %all-gather.8.cloned.1.call-update) | async-done | bytes 2359312 | tf_op jit(solution)/shard_map/all_gather | solution.py:58
  68.8 1.9 copy.68
  70.7 2.2 gather_fusion
  72.9 2.1 copy.58
  75.2 1.5 fusion.8
  77.0 0.9 pad_maximum_fusion.1
  78.0 29.3 %all-gather.14.cloned.1.call-done = bf16[2048,384]{1,0:T(8,128)(2,1)} async-done(((bf16[512,384]{1,0:T(8,128)(2,1)}), bf16[2048,384]{1,0:T(8,128)(2,1)}) %all-gather.14.cloned.1.call-update) | async-done | bytes 1572880 | tf_op jit(solution)/shard_map/all_gather | solution.py:57
  107.3 2.3 gather_fusion.2
  109.6 0.8 copy.54
  110.4 1.3 broadcast_select_fusion.1
  111.8 0.6 gather_fusion.8
  112.5 0.6 gather_fusion.9
  113.7 75.4 %all-gather.18.cloned.1.call-done = bf16[2048,1024]{1,0:T(8,128)(2,1)} async-done(((bf16[512,1024]{1,0:T(8,128)(2,1)}), bf16[2048,1024]{1,0:T(8,128)(2,1)}) %all-gather.18.cloned.1.call-update) | async-done | bytes 4194320 | tf_op jit(solution)/shard_map/all_gather | solution.py:60
  189.1 4.9 gather_fusion.3
  194.1 4.9 broadcast_select_fusion
  198.9 12.8 %all-gather.12.cloned.1.call-done = bf16[512,2048]{1,0:T(8,128)(2,1)} async-done(((bf16[512,512]{1,0:T(8,128)(2,1)}), bf16[512,2048]{1,0:T(8,128)(2,1)}) %all-gather.12.cloned.1.call-update) | async-done | bytes 2097168 | tf_op jit(solution)/shard_map/all_gather | solution.py:68
  211.7 25.8 %all-gather.10.cloned.1.call-done = bf16[2,1024,576]{1,2,0:T(8,128)(2,1)} async-done(((bf16[2,256,576]{1,2,0:T(8,128)(2,1)}), bf16[2,1024,576]{1,2,0:T(8,128)(2,1)}) %all-gather.10.cloned.1.call-update) | async-done | bytes 2359312 | tf_op jit(solution)/shard_map/all_gather | solution.py:88
  237.5 10.7 %convolution_convert_fusion = bf16[2,1024,2048]{2,1,0:T(8,128)(2,1)} fusion(bf16[2,1024,576]{1,2,0:T(8,128)(2,1)} %all-gather.10.cloned.1.call-done, bf16[512,2048]{1,0:T(8,128)(2,1)} %all-gather.12.cloned.1.call-done), kind=kOutput, calls=%fused_computation.20 | convolution fusion | flops 4299161600 | bytes 12582912 | tf_op jit(solution)/shard_map/dot_general | solution.py:91
  248.2 14.5 %reshape.344 = bf16[2,1024,8,2,128]{4,3,2,1,0:T(2,128)(2,1)} reshape(bf16[2,1024,2048]{2,1,0:T(8,128)(2,1)} %convolution_convert_fusion) | data formatting | bytes 16777216 | tf_op jit(solution)/shard_map/reshape | solution.py:95
  262.6 17.5 %fusion.36 = (bf16[2,1024,8,1,128]{4,3,2,1,0:T(2,128)(2,1)}, bf16[2,1024,8,1,128]{4,3,2,1,0:T(2,128)(2,1)}) fusion(bf16[2,1024,8,2,128]{4,3,2,1,0:T(2,128)(2,1)} %reshape.344), kind=kLoop, calls=%fused_computation.93 | loop fusion | bytes 16777216 | tf_op jit(solution)/shard_map/slice | solution.py:97
  280.1 20.2 %copy.55 = bf16[2,1024,8,1,128]{1,4,2,0,3:T(8,128)(2,1)} copy(bf16[2,1024,8,1,128]{4,3,2,1,0:T(2,128)(2,1)} %get-tuple-element.9) | data formatting | bytes 8388608
  300.3 5.7 fusion.13
  306.0 1.6 copy-done.8
  307.8 9.1 fusion.22
  316.9 17.3 %fusion.37 = (f32[2,8,256]{2,1,0:T(8,128)S(1)}, f32[2,8,256,1024]{3,2,1,0:T(8,128)}) fusion(f32[2,1024,256,8]{1,2,3,0:T(8,128)} %fusion.22, pred[2,256,1024]{2,1,0:T(8,128)(4,1)S(1)} %broadcast_and_fusion, bf16[2,1024,8,1,128]{4,3,2,1,0:T(2,128)(2,1)} %get-tuple-element.10, f32[2,256,8,192]{1,3,2,0:T(8,128)} %copy-done.8), kind=kOutput, calls=%fused_computation.94 | convolution fusion | flops 1094714368 | bytes 43532288 | tf_op jit(solution)/shard_map/sub | solution.py:113
  334.2 8.8 fusion.18
  343.0 4.4 fusion.38
  347.4 9.2 convert_element_type.85
  356.7 45.0 %reduce-scatter.2.cloned.1.call-done = f32[2,256,1024]{2,1,0:T(8,128)} async-done(((f32[2,256,2048]{2,1,0:T(8,128)}), f32[2,256,1024]{2,1,0:T(8,128)}) %reduce-scatter.2.cloned.1.call-update) | async-done | bytes 2097168 | tf_op jit(solution)/shard_map/reduce_scatter | solution.py:124
  401.7 2.0 add_convert_fusion
  404.0 11.2 %psum.14 = f32[2,2048]{1,0:T(2,128)S(1)} all-reduce(f32[2,2048]{1,0:T(2,128)S(1)} %bitcast_dynamic-update-slice_fusion), channel_id=1, replica_groups=mesh['dp'=4,'tx'=2,'ty'=4] {'ty'}, use_global_device_ids=true, to_apply=%region_6.8 | all-reduce | flops 4096 | bytes 32768 | tf_op jit(solution)/shard_map/psum | solution.py:132
  415.1 7.2 psum.15
  422.5 474.0 %all-gather.20.cloned.1.call-done = bf16[2048,7168]{1,0:T(8,128)(2,1)} async-done(((bf16[512,7168]{1,0:T(8,128)(2,1)}), bf16[2048,7168]{1,0:T(8,128)(2,1)}) %all-gather.20.cloned.1.call-update) | async-done | bytes 29360144 | tf_op jit(solution)/shard_map/all_gather | solution.py:134
  896.5 20.0 %fusion.35 = (bf16[4,512,1792]{2,1,0:T(8,128)(2,1)}, bf16[4,512,1792]{2,1,0:T(8,128)(2,1)}, bf16[4,512,1792]{2,1,0:T(8,128)(2,1)}, bf16[4,512,1792]{2,1,0:T(8,128)(2,1)}) fusion(bf16[4,512,7168]{2,1,0:T(8,128)(2,1)} %bitcast.74), kind=kLoop, calls=%fused_computation.92 | loop fusion | bytes 58720256 | tf_op jit(solution)/shard_map/jit(_take)/gather | solution.py:54
  916.6 7.1 gather_fusion.7
  923.7 7.0 gather_fusion.6
  930.7 7.1 gather_fusion.5
  937.8 7.1 gather_fusion.4
  944.9 20.2 %pad_maximum_fusion = bf16[4,512,7168]{2,1,0:T(8,128)(2,1)} fusion(bf16[4,512,1792]{2,1,0:T(8,128)(2,1)} %gather_fusion.7, bf16[4,512,1792]{2,1,0:T(8,128)(2,1)} %gather_fusion.6, bf16[4,512,1792]{2,1,0:T(8,128)(2,1)} %gather_fusion.5, bf16[4,512,1792]{2,1,0:T(8,128)(2,1)} %gather_fusion.4), kind=kLoop, calls=%fused_computation.12 | loop fusion | flops 117440512 | bytes 58720256
  965.1 20.3 %bitcast_select_fusion = bf16[2048,7168]{1,0:T(8,128)(2,1)} fusion(bf16[4,512,7168]{2,1,0:T(8,128)(2,1)} %pad_maximum_fusion, pred[2048]{0:T(1024)(128)(4,1)S(1)} %bitcast.86), kind=kLoop, calls=%fused_computation.13 | loop fusion | flops 14680064 | bytes 58722304 | tf_op jit(solution)/shard_map/jit(_take)/select_n | solution.py:54
  985.4 12.0 %fusion.26 = f32[2,7168]{1,0:T(2,128)} fusion(bf16[2048,7168]{1,0:T(8,128)(2,1)} %bitcast_select_fusion, f32[2,2048]{1,0:T(2,128)S(1)} %psum.15, f32[2]{0:T(128)S(1)} %add_rsqrt_fusion.2, f32[2048]{0:T(1024)S(1)} %copy-done.10), kind=kOutput, calls=%fused_computation.62 | convolution fusion | flops 58732544 | bytes 29442056 | tf_op jit(solution)/shard_map/dot_general | solution.py:135
  (77 shorter events, 3.2 us)
Async XLA Ops:
  7.2 104.6 %copy-start = (s32[8]{0:T(128)S(1)}, s32[8]{0:T(128)}, u32[]{:S(2)}) copy-start(s32[8]{0:T(128)} %param.16) | copy-start | bytes 100
  7.2 7.3 copy-start.9
  7.2 7.4 copy-start.13
  7.2 61.6 %all-gather.8.cloned.1.call-start = ((), (), s32[]{:S(2)}) async-start(), calls=%async_computation.1 | async-start | bytes 2949120 | tf_op jit(solution)/shard_map/all_gather | solution.py:58
  9.5 97.8 %all-gather.14.cloned.1.call-start = ((), (), s32[]{:S(2)}) async-start(), calls=%async_computation.4 | async-start | bytes 1966080 | tf_op jit(solution)/shard_map/all_gather | solution.py:57
  11.5 29.6 %copy-start.3 = (bf16[2,256,2048]{2,1,0:T(8,128)(2,1)S(1)}, bf16[2,256,2048]{2,1,0:T(8,128)(2,1)}, u32[]{:S(2)}) copy-start(bf16[2,256,2048]{2,1,0:T(8,128)(2,1)} %param.14) | copy-start | bytes 6291460
  11.5 177.6 %all-gather.18.cloned.1.call-start = ((), (), s32[]{:S(2)}) async-start(), calls=%async_computation.6 | async-start | bytes 5242880 | tf_op jit(solution)/shard_map/all_gather | solution.py:60
  14.5 197.2 %all-gather.12.cloned.1.call-start = ((), (), s32[]{:S(2)}) async-start(), calls=%async_computation.3 | async-start | bytes 2621440 | tf_op jit(solution)/shard_map/all_gather | solution.py:68
  41.0 196.5 %all-gather.10.cloned.1.call-start = ((), (), s32[]{:S(2)}) async-start(), calls=%async_computation.2 | async-start | bytes 2949120 | tf_op jit(solution)/shard_map/all_gather | solution.py:88
  70.7 4.3 copy-start.12
  72.9 2.3 copy-start.4
  75.2 1.7 copy-start.11
  77.9 222.3 %all-gather.16.cloned.1.call-start = ((), (), s32[]{:S(2)}) async-start(), calls=%async_computation.5 | async-start | bytes 7864320 | tf_op jit(solution)/shard_map/all_gather | solution.py:67
  109.6 2.8 copy-start.2
  111.7 290.0 %reduce-scatter.2.cloned.1.call-start = ((), (), s32[]{:S(2)}) async-start(), calls=%async_computation.7 | async-start | bytes 6291456 | tf_op jit(solution)/shard_map/reduce_scatter | solution.py:124
  280.1 20.2 %copy-start.5 = (bf16[2,256,2048]{2,1,0:T(8,128)(2,1)S(1)}, bf16[2,256,2048]{2,1,0:T(8,128)(2,1)}, u32[]{:S(2)}) copy-start(bf16[2,256,2048]{2,1,0:T(8,128)(2,1)} %param.14) | copy-start | bytes 6291460
  306.0 1.6 copy-start.8
  334.2 8.8 copy-start.7
  347.4 549.2 %all-gather.20.cloned.1.call-start = ((), (), s32[]{:S(2)}) async-start(), calls=%async_computation.8 | async-start | bytes 36700160 | tf_op jit(solution)/shard_map/all_gather | solution.py:134
  403.7 512.9 %copy-start.6 = (bf16[2,256,1024]{2,1,0:T(8,128)(2,1)}, bf16[2,256,1024]{2,1,0:T(8,128)(2,1)S(1)}, u32[]{:S(2)}) copy-start(bf16[2,256,1024]{2,1,0:T(8,128)(2,1)S(1)} %add_convert_fusion) | copy-start | bytes 3145732
  965.0 20.3 %copy-start.10 = (f32[2048]{0:T(1024)S(1)}, f32[2048]{0:T(1024)}, u32[]{:S(2)}) copy-start(f32[2048]{0:T(1024)} %param.20) | copy-start | bytes 24580
  985.4 12.0 %copy-start.1 = (s32[8]{0:T(128)S(1)}, s32[8]{0:T(128)}, u32[]{:S(2)}) copy-start(s32[8]{0:T(128)} %param.16) | copy-start | bytes 100
Sparse Core Ops, SparseCore 0:
  9.6 59.1 all-gather.7
  70.4 36.8 all-gather.13
  109.5 79.6 all-gather.17
  190.5 21.1 all-gather.11
  213.1 24.3 all-gather.9
  238.9 46.3 all-gather.15
  347.5 54.1 reduce-scatter.1
  403.4 493.1 all-gather.19
